TPU v7x, 32 devices: a whole 2x2x4 slice. The times are simulated.
32 devices in a mesh: gx: 4 (over z), gy: 8 (over y, x, core).
Axes of the slice: x: 2, y: 2, z: 4, core: 2. Of those that a mesh axis runs over, the one named last changes fastest.
Arguments:
- conductivity: bfloat16 [2, 1024, 4096], P(None, 'gy', 'gx'), may hold values from 0.099609375 to 1.59375
Outputs:
- coarse_stencil: float32 [9, 8, 64, 2048], P(None, 'gy', 'gx')
All inputs are finite; a program needn't handle non-finite values.
Results may differ from a plain program's by a relative error of at most 0.0003.
Values may be sent and summed in bfloat16 or wider, within the bound.
A program may use at most 64 MiB of HBM per device.

v0:
```python
from functools import partial
import jax
import jax.numpy as jnp
from jax import lax
from jax.sharding import PartitionSpec as P


def with_halo(cells, sides, width):
    for axis, dim in sides:
        count = lax.axis_size(axis)
        ends = count - 1
        head = lax.slice_in_dim(cells, 0, width, axis=dim)
        tail = lax.slice_in_dim(cells, cells.shape[dim] - width, cells.shape[dim], axis=dim)
        cells = jnp.concatenate(
            [
                lax.ppermute(tail, axis, [(i, (i + 1) % count) for i in range(ends)]),
                cells,
                lax.ppermute(head, axis, [((i + 1) % count, i) for i in range(ends)]),
            ],
            axis=dim,
        )
    return cells


def harmonic(first, second):
    return 2.0 * first * second / (first + second)


def prepare_window(extended, row_start, col_start, rows_all, cols_all, used_rows, used_cols):
    conduct = extended.astype(jnp.float32)
    ext_rows = conduct.shape[1]
    ext_cols = conduct.shape[2]
    row_places = jnp.arange(ext_rows, dtype=jnp.int32)
    col_places = jnp.arange(ext_cols, dtype=jnp.int32)
    row_ids = row_start - 2 + row_places
    col_ids = col_start - 2 + col_places
    row_inside = (row_ids >= 0) & (row_ids < rows_all) & (row_places < used_rows)
    col_inside = (col_ids >= 0) & (col_ids < cols_all) & (col_places < used_cols)
    inside = row_inside[:, None] & col_inside[None, :]
    safe_values = jnp.where(inside[None], conduct, 1.0)
    east_face = jnp.where(
        jnp.roll(inside, -1, 1)[None],
        harmonic(safe_values, jnp.roll(safe_values, -1, 2)),
        safe_values,
    )
    west_face = jnp.where(
        jnp.roll(inside, 1, 1)[None],
        harmonic(safe_values, jnp.roll(safe_values, 1, 2)),
        safe_values,
    )
    north_face = jnp.where(
        jnp.roll(inside, -1, 0)[None],
        harmonic(safe_values, jnp.roll(safe_values, -1, 1)),
        safe_values,
    )
    south_face = jnp.where(
        jnp.roll(inside, 1, 0)[None],
        harmonic(safe_values, jnp.roll(safe_values, 1, 1)),
        safe_values,
    )
    vertical = harmonic(safe_values[0], safe_values[1])
    centre = east_face + west_face + north_face + south_face + vertical[None] + safe_values
    col_east = east_face[0] + east_face[1]
    col_west = west_face[0] + west_face[1]
    row_north = north_face[0] + north_face[1]
    row_south = south_face[0] + south_face[1]
    left_weight = col_west / (col_west + col_east)
    right_weight = col_east / (col_west + col_east)
    south_weight = row_south / (row_south + row_north)
    north_weight = row_north / (row_south + row_north)
    odd_rows = (row_ids % 2 == 1)[:, None]
    odd_cols = (col_ids % 2 == 1)[None, :]
    even_point = inside & (row_ids % 2 == 0)[:, None] & (col_ids % 2 == 0)[None, :]
    row_class = (row_ids // 2 % 3)[:, None]
    col_class = (col_ids // 2 % 3)[None, :]
    return (
        inside,
        odd_rows,
        odd_cols,
        even_point,
        row_class,
        col_class,
        east_face,
        west_face,
        north_face,
        south_face,
        vertical,
        centre,
        left_weight,
        right_weight,
        south_weight,
        north_weight,
    )


def probe_rows(prepared, local_rows, colour):
    (
        inside,
        odd_rows,
        odd_cols,
        even_point,
        row_class,
        col_class,
        east_face,
        west_face,
        north_face,
        south_face,
        vertical,
        centre,
        left_weight,
        right_weight,
        south_weight,
        north_weight,
    ) = prepared
    chosen = even_point & (row_class == colour // 3) & (col_class == colour % 3)
    probe_field = chosen.astype(jnp.float32)
    along_x = jnp.where(
        odd_cols,
        left_weight * jnp.roll(probe_field, 1, 1) + right_weight * jnp.roll(probe_field, -1, 1),
        probe_field,
    )
    fine_field = jnp.where(
        odd_rows,
        south_weight * jnp.roll(along_x, 1, 0) + north_weight * jnp.roll(along_x, -1, 0),
        along_x,
    )
    fine_field = jnp.where(inside, fine_field, 0.0)
    applied = (
        centre * fine_field
        - east_face * jnp.roll(fine_field, -1, 1)
        - west_face * jnp.roll(fine_field, 1, 1)
        - north_face * jnp.roll(fine_field, -1, 0)
        - south_face * jnp.roll(fine_field, 1, 0)
        - vertical * fine_field
    )
    folded = jnp.where(inside, applied[0] + applied[1], 0.0)
    rows_done = (
        folded + jnp.roll(south_weight * folded, -1, 0) + jnp.roll(north_weight * folded, 1, 0)
    )
    cols_done = (
        rows_done
        + jnp.roll(left_weight * rows_done, -1, 1)
        + jnp.roll(right_weight * rows_done, 1, 1)
    )
    width = cols_done.shape[1]
    kept = cols_done[2 : 2 + local_rows].reshape(local_rows // 2, 2, width)
    return kept[:, 0]


def by_offset(colours, row_first, col_first):
    count_rows = colours.shape[1]
    count_cols = colours.shape[2]
    coarse_rows = row_first + jnp.arange(count_rows, dtype=jnp.int32)
    coarse_cols = col_first + jnp.arange(count_cols, dtype=jnp.int32)
    fields = []
    for step_row in (-1, 0, 1):
        for step_col in (-1, 0, 1):
            row_group = (coarse_rows + step_row) % 3
            col_group = (coarse_cols + step_col) % 3
            selected = jnp.zeros((count_rows, count_cols), jnp.float32)
            for colour in range(9):
                chosen = (row_group == colour // 3)[:, None] & (col_group == colour % 3)[None, :]
                selected = jnp.where(chosen, colours[colour], selected)
            fields.append(selected)
    return jnp.stack(fields)


def shards(conductivity):
    local_rows = conductivity.shape[1]
    local_cols = conductivity.shape[2]
    row_start = lax.axis_index("gy") * local_rows
    col_start = lax.axis_index("gx") * local_cols
    rows_all = local_rows * lax.axis_size("gy")
    cols_all = local_cols * lax.axis_size("gx")
    extended = with_halo(conductivity, (("gx", 2), ("gy", 1)), 2)
    used_rows = local_rows + 4
    used_cols = local_cols + 4
    row_fill = -used_rows % 8
    col_fill = -used_cols % 128
    aligned = jnp.pad(extended, ((0, 0), (0, row_fill), (0, col_fill)))
    prepared = prepare_window(
        aligned, row_start, col_start, rows_all, cols_all, used_rows, used_cols
    )
    row_picked = lax.map(partial(probe_rows, prepared, local_rows), jnp.arange(9, dtype=jnp.int32))
    width = row_picked.shape[2]
    half_cols = local_cols // 2
    picker = (
        jnp.arange(width, dtype=jnp.int32)[:, None]
        == 2 + 2 * jnp.arange(half_cols, dtype=jnp.int32)[None, :]
    ).astype(jnp.float32)
    flat_rows = row_picked.reshape(9 * (local_rows // 2), width)
    colours = jnp.dot(
        flat_rows, picker, precision=lax.Precision.HIGHEST, preferred_element_type=jnp.float32
    )
    colours = colours.reshape(9, local_rows // 2, half_cols)
    stencil = by_offset(colours, row_start // 2, col_start // 2)
    moved = lax.all_to_all(stencil, "gx", split_axis=1, concat_axis=2, tiled=True)
    return moved[:, None]


def solution(mesh):
    in_specs = (P(None, "gy", "gx"),)
    out_specs = P(None, "gy", "gx", None)
    return jax.shard_map(shards, mesh=mesh, in_specs=in_specs, out_specs=out_specs, check_vma=False)
```

profile of v0, /device:TPU:4, one launch (start us, length us, event | category | flops | bytes accessed | tf_op | source)
XLA Modules:
  0.0 210.9 jit_solution(8876209915577884419)
XLA Ops:
  1.0 3.5 %collective-permute-start = (bf16[2,128,2]{2,1,0:T(8,128)(2,1)S(1)}, bf16[2,128,2]{2,1,0:T(8,128)(2,1)S(1)}, u32[]{:S(2)}, u32[]{:S(2)}) collective-permute-start(bf16[2,128,2]{2,1,0:T(8,128)(2,1)S(1)} %get-tuple-element.442), channel_id=1, source_target_pairs={{0,8},{8,16},{16,24},{1,9},{9,17},{17,25},{2,10},{10,18},{18,26},{... | collective-permute-start | bytes 3080 | tf_op jit(solution)/shard_map/ppermute | solution.py:16
  4.5 1.3 collective-permute-start.1
  7.1 3.5 %collective-permute-done.1 = bf16[2,128,2]{2,1,0:T(8,128)(2,1)S(1)} collective-permute-done((bf16[2,128,2]{2,1,0:T(8,128)(2,1)S(1)}, bf16[2,128,2]{2,1,0:T(8,128)(2,1)S(1)}, u32[]{:S(2)}, u32[]{:S(2)}) %collective-permute-start.1) | collective-permute-done | bytes 1056 | tf_op jit(solution)/shard_map/ppermute | solution.py:18
  11.3 1.9 collective-permute-start.2
  13.2 4.5 %collective-permute-start.3 = (bf16[2,2,1028]{2,1,0:T(2,128)(2,1)S(1)}, bf16[2,2,1028]{2,1,0:T(2,128)(2,1)S(1)}, u32[]{:S(2)}, u32[]{:S(2)}) collective-permute-start(bf16[2,2,1028]{2,1,0:T(2,128)(2,1)S(1)} %get-tuple-element.440), channel_id=1, source_target_pairs={{1,0},{2,1},{3,2},{4,3},{5,4},{6,5},{7,6},{9,8},{10,9},{11,10},{12... | collective-permute-start | bytes 24680 | tf_op jit(solution)/shard_map/ppermute | solution.py:18
  17.8 1.3 collective-permute-done.3
  21.1 4.2 %add_add_fusion = (f32[2,136,1152]{2,1,0:T(8,128)}, f32[2,136,1152]{2,1,0:T(8,128)S(1)}, f32[2,136,1152]{2,1,0:T(8,128)S(1)}, f32[2,136,1152]{2,1,0:T(8,128)S(1)}, f32[2,136,1152]{2,1,0:T(8,128)S(1)}) fusion(f32[136,1152]{1,0:T(8,128)S(1)} %divide_bitcast_fusion, pred[136,1152]{1,0:T(8,128)(4,1)S(1)} %broadcast_and_fusion, ...), kind=kLoop, calls=%fused_computation.66 | loop fusion | flops 13160448 | bytes 13233216 | tf_op jit(solution)/shard_map/add | solution.py:62
  27.6 121.1 %while.14 = (s32[]{:T(128)}, f32[9,64,1152]{2,1,0:T(8,128)}, s32[9]{0:T(128)S(1)}, f32[136,1152]{1,0:T(8,128)S(1)}, f32[136,1152]{1,0:T(8,128)S(1)}, /*index=5*/...) while((s32[]{:T(128)}, f32[9,64,1152]{2,1,0:T(8,128)}, ...), condition=%wide.region_1.2_spmd.clone.clone, body=%wide.region_0.1_spmd.clone.clone.sunk | while | flops 10339566 | bytes 78140304 | solution.py:184
  31.2 1.4 fusion.104
  37.9 1.2 reshape.701
  39.1 1.3 slice_bitcast_fusion.2
  44.6 1.4 fusion.104
  52.5 1.3 slice_bitcast_fusion.2
  58.1 1.4 fusion.104
  66.0 1.3 slice_bitcast_fusion.2
  71.5 1.4 fusion.104
  78.2 1.2 reshape.701
  79.4 1.3 slice_bitcast_fusion.2
  85.0 1.4 fusion.104
  92.9 1.3 slice_bitcast_fusion.2
  98.4 1.4 fusion.104
  105.1 1.2 reshape.701
  106.3 1.3 slice_bitcast_fusion.2
  111.9 1.4 fusion.104
  119.8 1.3 slice_bitcast_fusion.2
  125.4 1.4 fusion.104
  133.2 1.3 slice_bitcast_fusion.2
  138.8 1.4 fusion.104
  146.7 1.3 slice_bitcast_fusion.2
  148.7 4.3 %fusion.23 = f32[576,512]{1,0:T(8,128)S(1)} fusion(f32[576,1152]{1,0:T(8,128)} %bitcast.88, s32[512]{0:T(512)S(1)} %multiply_add_fusion), kind=kOutput, calls=%fused_computation.55 | convolution fusion | flops 4077453312 | bytes 3835904 | tf_op jit(solution)/shard_map/dot_general | solution.py:192
  155.7 52.7 %all_to_all.15 = f32[9,64,512]{2,0,1:T(8,128)S(1)} all-to-all(f32[9,64,512]{2,0,1:T(8,128)S(1)} %copy.7), channel_id=1, replica_groups=mesh['gx'=4,'gy'=8] {'gx'}, dimensions={1} | all-to-all | bytes 2359296 | tf_op jit(solution)/shard_map/all_to_all | solution.py:197
  209.1 1.8 broadcast_in_dim.97
  (425 shorter events, 86.9 us)
Async XLA Ops:
  1.0 6.1 %collective-permute-start = (bf16[2,128,2]{2,1,0:T(8,128)(2,1)S(1)}, bf16[2,128,2]{2,1,0:T(8,128)(2,1)S(1)}, u32[]{:S(2)}, u32[]{:S(2)}) collective-permute-start(bf16[2,128,2]{2,1,0:T(8,128)(2,1)S(1)} %get-tuple-element.442), channel_id=1, source_target_pairs={{0,8},{8,16},{16,24},{1,9},{9,17},{17,25},{2,10},{10,18},{18,26},{... | collective-permute-start | bytes 3080 | tf_op jit(solution)/shard_map/ppermute | solution.py:16
  4.5 6.2 %collective-permute-start.1 = (bf16[2,128,2]{2,1,0:T(8,128)(2,1)S(1)}, bf16[2,128,2]{2,1,0:T(8,128)(2,1)S(1)}, u32[]{:S(2)}, u32[]{:S(2)}) collective-permute-start(bf16[2,128,2]{2,1,0:T(8,128)(2,1)S(1)} %get-tuple-element.441), channel_id=1, source_target_pairs={{8,0},{16,8},{24,16},{9,1},{17,9},{25,17},{10,2},{18,10},{26,18},{... | collective-permute-start | bytes 3080 | tf_op jit(solution)/shard_map/ppermute | solution.py:18
  5.9 4.7 %copy-start.9 = (bf16[2,128,1024]{2,1,0:T(8,128)(2,1)S(1)}, bf16[2,128,1024]{2,1,0:T(8,128)(2,1)}, u32[]{:S(2)}) copy-start(bf16[2,128,1024]{2,1,0:T(8,128)(2,1)} %param.3) | copy-start | bytes 1572868
  11.3 6.5 %collective-permute-start.2 = (bf16[2,2,1028]{2,1,0:T(2,128)(2,1)S(1)}, bf16[2,2,1028]{2,1,0:T(2,128)(2,1)S(1)}, u32[]{:S(2)}, u32[]{:S(2)}) collective-permute-start(bf16[2,2,1028]{2,1,0:T(2,128)(2,1)S(1)} %get-tuple-element.439), channel_id=1, source_target_pairs={{0,1},{1,2},{2,3},{3,4},{4,5},{5,6},{6,7},{8,9},{9,10},{10,11},{11... | collective-permute-start | bytes 24680 | tf_op jit(solution)/shard_map/ppermute | solution.py:16
  13.2 5.9 %collective-permute-start.3 = (bf16[2,2,1028]{2,1,0:T(2,128)(2,1)S(1)}, bf16[2,2,1028]{2,1,0:T(2,128)(2,1)S(1)}, u32[]{:S(2)}, u32[]{:S(2)}) collective-permute-start(bf16[2,2,1028]{2,1,0:T(2,128)(2,1)S(1)} %get-tuple-element.440), channel_id=1, source_target_pairs={{1,0},{2,1},{3,2},{4,3},{5,4},{6,5},{7,6},{9,8},{10,9},{11,10},{12... | collective-permute-start | bytes 24680 | tf_op jit(solution)/shard_map/ppermute | solution.py:18
  25.3 2.0 copy-start.4
  25.3 2.3 %copy-start.6 = (f32[2,136,1152]{2,1,0:T(8,128)}, f32[2,136,1152]{2,1,0:T(8,128)S(1)}, u32[]{:S(2)}) copy-start(f32[2,136,1152]{2,1,0:T(8,128)S(1)} %get-tuple-element.647) | copy-start | bytes 3760132
  33.3 1.9 copy-start.7
  33.4 2.2 %copy-start.1 = (f32[2,136,1152]{2,1,0:T(8,128)S(1)}, f32[2,136,1152]{2,1,0:T(8,128)}, u32[]{:S(2)}) copy-start(f32[2,136,1152]{2,1,0:T(8,128)} %get-tuple-element.698) | copy-start | bytes 3760132 | tf_op jit(solution)/shard_map/while
  33.4 2.5 %copy-start.3 = (f32[2,136,1152]{2,1,0:T(8,128)S(1)}, f32[2,136,1152]{2,1,0:T(8,128)}, u32[]{:S(2)}) copy-start(f32[2,136,1152]{2,1,0:T(8,128)} %get-tuple-element.699) | copy-start | bytes 3760132 | tf_op jit(solution)/shard_map/while
  46.7 1.9 copy-start.7
  46.8 2.2 %copy-start.1 = (f32[2,136,1152]{2,1,0:T(8,128)S(1)}, f32[2,136,1152]{2,1,0:T(8,128)}, u32[]{:S(2)}) copy-start(f32[2,136,1152]{2,1,0:T(8,128)} %get-tuple-element.698) | copy-start | bytes 3760132 | tf_op jit(solution)/shard_map/while
  46.9 2.5 %copy-start.3 = (f32[2,136,1152]{2,1,0:T(8,128)S(1)}, f32[2,136,1152]{2,1,0:T(8,128)}, u32[]{:S(2)}) copy-start(f32[2,136,1152]{2,1,0:T(8,128)} %get-tuple-element.699) | copy-start | bytes 3760132 | tf_op jit(solution)/shard_map/while
  60.2 1.9 copy-start.7
  60.3 2.2 %copy-start.1 = (f32[2,136,1152]{2,1,0:T(8,128)S(1)}, f32[2,136,1152]{2,1,0:T(8,128)}, u32[]{:S(2)}) copy-start(f32[2,136,1152]{2,1,0:T(8,128)} %get-tuple-element.698) | copy-start | bytes 3760132 | tf_op jit(solution)/shard_map/while
  60.3 2.5 %copy-start.3 = (f32[2,136,1152]{2,1,0:T(8,128)S(1)}, f32[2,136,1152]{2,1,0:T(8,128)}, u32[]{:S(2)}) copy-start(f32[2,136,1152]{2,1,0:T(8,128)} %get-tuple-element.699) | copy-start | bytes 3760132 | tf_op jit(solution)/shard_map/while
  73.6 1.9 copy-start.7
  73.7 2.2 %copy-start.1 = (f32[2,136,1152]{2,1,0:T(8,128)S(1)}, f32[2,136,1152]{2,1,0:T(8,128)}, u32[]{:S(2)}) copy-start(f32[2,136,1152]{2,1,0:T(8,128)} %get-tuple-element.698) | copy-start | bytes 3760132 | tf_op jit(solution)/shard_map/while
  73.8 2.5 %copy-start.3 = (f32[2,136,1152]{2,1,0:T(8,128)S(1)}, f32[2,136,1152]{2,1,0:T(8,128)}, u32[]{:S(2)}) copy-start(f32[2,136,1152]{2,1,0:T(8,128)} %get-tuple-element.699) | copy-start | bytes 3760132 | tf_op jit(solution)/shard_map/while
  87.1 1.9 copy-start.7
  87.2 2.2 %copy-start.1 = (f32[2,136,1152]{2,1,0:T(8,128)S(1)}, f32[2,136,1152]{2,1,0:T(8,128)}, u32[]{:S(2)}) copy-start(f32[2,136,1152]{2,1,0:T(8,128)} %get-tuple-element.698) | copy-start | bytes 3760132 | tf_op jit(solution)/shard_map/while
  87.2 2.5 %copy-start.3 = (f32[2,136,1152]{2,1,0:T(8,128)S(1)}, f32[2,136,1152]{2,1,0:T(8,128)}, u32[]{:S(2)}) copy-start(f32[2,136,1152]{2,1,0:T(8,128)} %get-tuple-element.699) | copy-start | bytes 3760132 | tf_op jit(solution)/shard_map/while
  100.5 1.9 copy-start.7
  100.6 2.2 %copy-start.1 = (f32[2,136,1152]{2,1,0:T(8,128)S(1)}, f32[2,136,1152]{2,1,0:T(8,128)}, u32[]{:S(2)}) copy-start(f32[2,136,1152]{2,1,0:T(8,128)} %get-tuple-element.698) | copy-start | bytes 3760132 | tf_op jit(solution)/shard_map/while
  100.7 2.5 %copy-start.3 = (f32[2,136,1152]{2,1,0:T(8,128)S(1)}, f32[2,136,1152]{2,1,0:T(8,128)}, u32[]{:S(2)}) copy-start(f32[2,136,1152]{2,1,0:T(8,128)} %get-tuple-element.699) | copy-start | bytes 3760132 | tf_op jit(solution)/shard_map/while
  114.1 2.2 %copy-start.1 = (f32[2,136,1152]{2,1,0:T(8,128)S(1)}, f32[2,136,1152]{2,1,0:T(8,128)}, u32[]{:S(2)}) copy-start(f32[2,136,1152]{2,1,0:T(8,128)} %get-tuple-element.698) | copy-start | bytes 3760132 | tf_op jit(solution)/shard_map/while
  114.1 2.5 %copy-start.3 = (f32[2,136,1152]{2,1,0:T(8,128)S(1)}, f32[2,136,1152]{2,1,0:T(8,128)}, u32[]{:S(2)}) copy-start(f32[2,136,1152]{2,1,0:T(8,128)} %get-tuple-element.699) | copy-start | bytes 3760132 | tf_op jit(solution)/shard_map/while
  127.6 2.2 %copy-start.1 = (f32[2,136,1152]{2,1,0:T(8,128)S(1)}, f32[2,136,1152]{2,1,0:T(8,128)}, u32[]{:S(2)}) copy-start(f32[2,136,1152]{2,1,0:T(8,128)} %get-tuple-element.698) | copy-start | bytes 3760132 | tf_op jit(solution)/shard_map/while
  127.6 2.5 %copy-start.3 = (f32[2,136,1152]{2,1,0:T(8,128)S(1)}, f32[2,136,1152]{2,1,0:T(8,128)}, u32[]{:S(2)}) copy-start(f32[2,136,1152]{2,1,0:T(8,128)} %get-tuple-element.699) | copy-start | bytes 3760132 | tf_op jit(solution)/shard_map/while
  140.9 1.9 copy-start.7
  141.0 2.2 %copy-start.1 = (f32[2,136,1152]{2,1,0:T(8,128)S(1)}, f32[2,136,1152]{2,1,0:T(8,128)}, u32[]{:S(2)}) copy-start(f32[2,136,1152]{2,1,0:T(8,128)} %get-tuple-element.698) | copy-start | bytes 3760132 | tf_op jit(solution)/shard_map/while
  141.0 2.5 %copy-start.3 = (f32[2,136,1152]{2,1,0:T(8,128)S(1)}, f32[2,136,1152]{2,1,0:T(8,128)}, u32[]{:S(2)}) copy-start(f32[2,136,1152]{2,1,0:T(8,128)} %get-tuple-element.699) | copy-start | bytes 3760132 | tf_op jit(solution)/shard_map/while
  (22 other events, 31.5 us)
where the time goes:
time: 212 us; the launch traced here: 211 us
  local copies, waits for them, and re-layouts  74.1 us (35%)
  blocking collectives  52.7 us (25%)
  other arithmetic  46.5 us (22%)
  loops' own time  16.9 us (8%)
  starting transfers between devices  11.2 us (5%)
  waiting for transfers between devices  4.81 us (2%)
  matrix products  4.33 us (2%)
    all_to_all x1, blocking collectives, shards(): lax.all_to_all(stencil, 'gx', split_axis=1, concat_axis=2, tiled=True)  52.7 us
    while x90, local copies, waits for them, and re-layouts  21.7 us
    another operation x1, loops' own time, shards(): lax.map(partial(probe_rows, prepared, local_rows), jnp.arange(9, dtype=jn...  16.9 us
    mul x9, other arithmetic, probe_rows(): vertical * fine_field  12.9 us
    broadcast_in_dim x9, local copies, waits for them, and re-layouts, shards(): lax.map(partial(probe_rows, prepared, local_rows), jnp.arange(9, dtype=jn...  11.4 us
    reshape x9, local copies, waits for them, and re-layouts, probe_rows(): kept = cols_done[2:2 + local_rows].reshape(local_rows // 2, 2, width)  10.5 us
    sub x9, other arithmetic, probe_rows(): centre * fine_field - east_face * jnp.roll(fine_field, -1, 1)  6.98 us
    dynamic_update_slice x9, local copies, waits for them, and re-layouts, shards(): lax.map(partial(probe_rows, prepared, local_rows), jnp.arange(9, dtype=jn...  6.72 us
  transfers between devices with their start and end apart: 4, of which 2 were waited for; matrix products, arithmetic and copies ran while one was open for 1% of the time, Pallas kernels for 0%

commit v1 on v0

--- a/solution.py
+++ b/solution.py
@@ -3,6 +3,29 @@
 import jax.numpy as jnp
 from jax import lax
 from jax.sharding import PartitionSpec as P
+
+
+def cut_along(value, dim, size):
+    dims = value.shape
+    blocks = value.reshape(*dims[:dim], size, dims[dim] // size, *dims[dim + 1 :])
+    return jnp.moveaxis(blocks, dim, 0)
+
+
+def joined_along(pieces, dim):
+    pieces = jnp.moveaxis(pieces, 0, dim)
+    shape = pieces.shape
+    return pieces.reshape(*shape[:dim], shape[dim] * shape[dim + 1], *shape[dim + 2 :])
+
+
+def sent_to_each(x, axis, split_dim, concat_dim):
+    length, place = (lax.axis_size(axis), lax.axis_index(axis))
+    blocks = cut_along(x, split_dim, length)
+    finished = [blocks[place]]
+    for hop in range(1, length):
+        sent = blocks[(place + hop) % length]
+        finished.append(lax.ppermute(sent, axis, [(i, (i + hop) % length) for i in range(length)]))
+    blocks = jnp.stack(finished)[(place - jnp.arange(length)) % length]
+    return joined_along(blocks, concat_dim)
 
 
 def with_halo(cells, sides, width):
@@ -194,7 +217,7 @@
     )
     colours = colours.reshape(9, local_rows // 2, half_cols)
     stencil = by_offset(colours, row_start // 2, col_start // 2)
-    moved = lax.all_to_all(stencil, "gx", split_axis=1, concat_axis=2, tiled=True)
+    moved = sent_to_each(stencil, "gx", 1, 2)
     return moved[:, None]
 
 

time: 212 us -> 192 us (0.906)
  the two profiles are of different devices: /device:TPU:4 before, /device:TPU:13 now
where the time goes in v1:
time: 192 us; the launch traced here: 191 us
  local copies, waits for them, and re-layouts  74.6 us (39%)
  other arithmetic  46.7 us (24%)
  waiting for transfers between devices  30.7 us (16%)
  loops' own time  19 us (10%)
  starting transfers between devices  14.9 us (8%)
  matrix products  4.33 us (2%)
    ppermute x3, waiting for transfers between devices, sent_to_each(): lax.ppermute(sent, axis, [(i, (i + hop) % length) for i in range(length)])  26.2 us
    while x90, local copies, waits for them, and re-layouts  21.7 us
    another operation x1, loops' own time, shards(): lax.map(partial(probe_rows, prepared, local_rows), jnp.arange(9, dtype=jn...  19 us
    mul x9, other arithmetic, probe_rows(): vertical * fine_field  12.9 us
    broadcast_in_dim x9, local copies, waits for them, and re-layouts, shards(): lax.map(partial(probe_rows, prepared, local_rows), jnp.arange(9, dtype=jn...  11.4 us
    reshape x9, local copies, waits for them, and re-layouts, probe_rows(): kept = cols_done[2:2 + local_rows].reshape(local_rows // 2, 2, width)  10.5 us
    ppermute x2, starting transfers between devices, with_halo(): lax.ppermute(tail, axis, [(i, (i + 1) % count) for i in range(ends)])  8.31 us
    sub x9, other arithmetic, probe_rows(): centre * fine_field - east_face * jnp.roll(fine_field, -1, 1)  6.98 us
  transfers between devices with their start and end apart: 7, of which 5 were waited for; matrix products, arithmetic and copies ran while one was open for 1% of the time, Pallas kernels for 0%

profile of v1, /device:TPU:13, one launch (start us, length us, event | category | flops | bytes accessed | tf_op | source)
XLA Modules:
  0.0 190.8 jit_solution(17581879478218706947)
XLA Ops:
  1.0 3.2 %collective-permute-start = (bf16[2,128,2]{2,1,0:T(8,128)(2,1)S(1)}, bf16[2,128,2]{2,1,0:T(8,128)(2,1)S(1)}, u32[]{:S(2)}, u32[]{:S(2)}) collective-permute-start(bf16[2,128,2]{2,1,0:T(8,128)(2,1)S(1)} %get-tuple-element.446), channel_id=1, source_target_pairs={{0,8},{8,16},{16,24},{1,9},{9,17},{17,25},{2,10},{10,18},{18,26},{... | collective-permute-start | bytes 3080 | tf_op jit(solution)/shard_map/ppermute | solution.py:39
  4.2 2.1 %collective-permute-start.1 = (bf16[2,128,2]{2,1,0:T(8,128)(2,1)S(1)}, bf16[2,128,2]{2,1,0:T(8,128)(2,1)S(1)}, u32[]{:S(2)}, u32[]{:S(2)}) collective-permute-start(bf16[2,128,2]{2,1,0:T(8,128)(2,1)S(1)} %get-tuple-element.445), channel_id=1, source_target_pairs={{8,0},{16,8},{24,16},{9,1},{17,9},{25,17},{10,2},{18,10},{26,18},{... | collective-permute-start | bytes 3080 | tf_op jit(solution)/shard_map/ppermute | solution.py:41
  7.6 1.6 collective-permute-done.1
  9.8 5.1 %collective-permute-start.2 = (bf16[2,2,1028]{2,1,0:T(2,128)(2,1)S(1)}, bf16[2,2,1028]{2,1,0:T(2,128)(2,1)S(1)}, u32[]{:S(2)}, u32[]{:S(2)}) collective-permute-start(bf16[2,2,1028]{2,1,0:T(2,128)(2,1)S(1)} %get-tuple-element.443), channel_id=1, source_target_pairs={{0,1},{1,2},{2,3},{3,4},{4,5},{5,6},{6,7},{8,9},{9,10},{10,11},{11... | collective-permute-start | bytes 24680 | tf_op jit(solution)/shard_map/ppermute | solution.py:39
  14.9 1.9 %collective-permute-start.3 = (bf16[2,2,1028]{2,1,0:T(2,128)(2,1)S(1)}, bf16[2,2,1028]{2,1,0:T(2,128)(2,1)S(1)}, u32[]{:S(2)}, u32[]{:S(2)}) collective-permute-start(bf16[2,2,1028]{2,1,0:T(2,128)(2,1)S(1)} %get-tuple-element.444), channel_id=1, source_target_pairs={{1,0},{2,1},{3,2},{4,3},{5,4},{6,5},{7,6},{9,8},{10,9},{11,10},{12... | collective-permute-start | bytes 24680 | tf_op jit(solution)/shard_map/ppermute | solution.py:41
  17.0 3.0 %collective-permute-done.3 = bf16[2,2,1028]{2,1,0:T(2,128)(2,1)S(1)} collective-permute-done((bf16[2,2,1028]{2,1,0:T(2,128)(2,1)S(1)}, bf16[2,2,1028]{2,1,0:T(2,128)(2,1)S(1)}, u32[]{:S(2)}, u32[]{:S(2)}) %collective-permute-start.3) | collective-permute-done | bytes 8256 | tf_op jit(solution)/shard_map/ppermute | solution.py:41
  22.0 4.1 %add_add_fusion = (f32[2,136,1152]{2,1,0:T(8,128)}, f32[2,136,1152]{2,1,0:T(8,128)S(1)}, f32[2,136,1152]{2,1,0:T(8,128)S(1)}, f32[2,136,1152]{2,1,0:T(8,128)S(1)}, f32[2,136,1152]{2,1,0:T(8,128)S(1)}) fusion(f32[136,1152]{1,0:T(8,128)S(1)} %divide_bitcast_fusion, pred[136,1152]{1,0:T(8,128)(4,1)S(1)} %broadcast_and_fusion, ...), kind=kLoop, calls=%fused_computation.67 | loop fusion | flops 13160448 | bytes 13233216 | tf_op jit(solution)/shard_map/add | solution.py:85
  28.5 123.6 %while.14 = (s32[]{:T(128)}, f32[9,64,1152]{2,1,0:T(8,128)}, s32[9]{0:T(128)S(1)}, f32[136,1152]{1,0:T(8,128)S(1)}, f32[136,1152]{1,0:T(8,128)S(1)}, /*index=5*/...) while((s32[]{:T(128)}, f32[9,64,1152]{2,1,0:T(8,128)}, ...), condition=%wide.region_1.2_spmd.clone.clone, body=%wide.region_0.1_spmd.clone.clone.sunk | while | flops 10339566 | bytes 78140304 | solution.py:207
  32.3 1.4 fusion.106
  40.2 1.3 slice_bitcast_fusion.2
  46.0 1.4 fusion.106
  53.9 1.3 slice_bitcast_fusion.2
  59.8 1.4 fusion.106
  67.7 1.3 slice_bitcast_fusion.2
  73.5 1.4 fusion.106
  81.4 1.3 slice_bitcast_fusion.2
  87.3 1.4 fusion.106
  95.2 1.3 slice_bitcast_fusion.2
  101.0 1.4 fusion.106
  108.9 1.3 slice_bitcast_fusion.2
  114.7 1.4 fusion.106
  122.6 1.3 slice_bitcast_fusion.2
  128.4 1.4 fusion.106
  136.3 1.3 slice_bitcast_fusion.2
  142.2 1.4 fusion.106
  150.1 1.3 slice_bitcast_fusion.2
  152.1 4.3 %fusion.23 = f32[576,512]{1,0:T(8,128)S(1)} fusion(f32[576,1152]{1,0:T(8,128)} %bitcast.103, s32[512]{0:T(512)S(1)} %multiply_add_fusion), kind=kOutput, calls=%fused_computation.56 | convolution fusion | flops 4077453312 | bytes 3835904 | tf_op jit(solution)/shard_map/dot_general | solution.py:215
  158.7 1.3 collective-permute-start.4
  161.3 6.2 %collective-permute-done.4 = f32[9,16,512]{2,1,0:T(8,128)S(1)} collective-permute-done((f32[9,16,512]{2,1,0:T(8,128)S(1)}, f32[9,16,512]{2,1,0:T(8,128)S(1)}, u32[]{:S(2)}, u32[]{:S(2)}) %collective-permute-start.4) | collective-permute-done | bytes 294944 | tf_op jit(solution)/shard_map/ppermute | solution.py:26
  167.4 18.0 %collective-permute-done.5 = f32[9,16,512]{2,1,0:T(8,128)S(1)} collective-permute-done((f32[9,16,512]{2,1,0:T(8,128)S(1)}, f32[9,16,512]{2,1,0:T(8,128)S(1)}, u32[]{:S(2)}, u32[]{:S(2)}) %collective-permute-start.5) | collective-permute-done | bytes 294944 | tf_op jit(solution)/shard_map/ppermute | solution.py:26
  185.5 2.0 %collective-permute-done.6 = f32[9,16,512]{2,1,0:T(8,128)S(1)} collective-permute-done((f32[9,16,512]{2,1,0:T(8,128)S(1)}, f32[9,16,512]{2,1,0:T(8,128)S(1)}, u32[]{:S(2)}, u32[]{:S(2)}) %collective-permute-start.6) | collective-permute-done | bytes 294944 | tf_op jit(solution)/shard_map/ppermute | solution.py:26
  189.0 1.8 broadcast_in_dim_reshape.3
  (443 shorter events, 92.3 us)
Async XLA Ops:
  1.0 6.7 %collective-permute-start = (bf16[2,128,2]{2,1,0:T(8,128)(2,1)S(1)}, bf16[2,128,2]{2,1,0:T(8,128)(2,1)S(1)}, u32[]{:S(2)}, u32[]{:S(2)}) collective-permute-start(bf16[2,128,2]{2,1,0:T(8,128)(2,1)S(1)} %get-tuple-element.446), channel_id=1, source_target_pairs={{0,8},{8,16},{16,24},{1,9},{9,17},{17,25},{2,10},{10,18},{18,26},{... | collective-permute-start | bytes 3080 | tf_op jit(solution)/shard_map/ppermute | solution.py:39
  4.2 5.0 %collective-permute-start.1 = (bf16[2,128,2]{2,1,0:T(8,128)(2,1)S(1)}, bf16[2,128,2]{2,1,0:T(8,128)(2,1)S(1)}, u32[]{:S(2)}, u32[]{:S(2)}) collective-permute-start(bf16[2,128,2]{2,1,0:T(8,128)(2,1)S(1)} %get-tuple-element.445), channel_id=1, source_target_pairs={{8,0},{16,8},{24,16},{9,1},{17,9},{25,17},{10,2},{18,10},{26,18},{... | collective-permute-start | bytes 3080 | tf_op jit(solution)/shard_map/ppermute | solution.py:41
  6.5 2.7 %copy-start.9 = (bf16[2,128,1024]{2,1,0:T(8,128)(2,1)S(1)}, bf16[2,128,1024]{2,1,0:T(8,128)(2,1)}, u32[]{:S(2)}) copy-start(bf16[2,128,1024]{2,1,0:T(8,128)(2,1)} %param.3) | copy-start | bytes 1572868
  9.8 7.1 %collective-permute-start.2 = (bf16[2,2,1028]{2,1,0:T(2,128)(2,1)S(1)}, bf16[2,2,1028]{2,1,0:T(2,128)(2,1)S(1)}, u32[]{:S(2)}, u32[]{:S(2)}) collective-permute-start(bf16[2,2,1028]{2,1,0:T(2,128)(2,1)S(1)} %get-tuple-element.443), channel_id=1, source_target_pairs={{0,1},{1,2},{2,3},{3,4},{4,5},{5,6},{6,7},{8,9},{9,10},{10,11},{11... | collective-permute-start | bytes 24680 | tf_op jit(solution)/shard_map/ppermute | solution.py:39
  14.9 5.0 %collective-permute-start.3 = (bf16[2,2,1028]{2,1,0:T(2,128)(2,1)S(1)}, bf16[2,2,1028]{2,1,0:T(2,128)(2,1)S(1)}, u32[]{:S(2)}, u32[]{:S(2)}) collective-permute-start(bf16[2,2,1028]{2,1,0:T(2,128)(2,1)S(1)} %get-tuple-element.444), channel_id=1, source_target_pairs={{1,0},{2,1},{3,2},{4,3},{5,4},{6,5},{7,6},{9,8},{10,9},{11,10},{12... | collective-permute-start | bytes 24680 | tf_op jit(solution)/shard_map/ppermute | solution.py:41
  26.1 2.0 %copy-start.4 = (f32[2,136,1152]{2,1,0:T(8,128)}, f32[2,136,1152]{2,1,0:T(8,128)S(1)}, u32[]{:S(2)}) copy-start(f32[2,136,1152]{2,1,0:T(8,128)S(1)} %get-tuple-element.650) | copy-start | bytes 3760132
  26.1 2.4 %copy-start.6 = (f32[2,136,1152]{2,1,0:T(8,128)}, f32[2,136,1152]{2,1,0:T(8,128)S(1)}, u32[]{:S(2)}) copy-start(f32[2,136,1152]{2,1,0:T(8,128)S(1)} %get-tuple-element.651) | copy-start | bytes 3760132
  34.4 1.9 copy-start.7
  34.5 2.2 %copy-start.1 = (f32[2,136,1152]{2,1,0:T(8,128)S(1)}, f32[2,136,1152]{2,1,0:T(8,128)}, u32[]{:S(2)}) copy-start(f32[2,136,1152]{2,1,0:T(8,128)} %get-tuple-element.702) | copy-start | bytes 3760132 | tf_op jit(solution)/shard_map/while
  34.5 2.5 %copy-start.3 = (f32[2,136,1152]{2,1,0:T(8,128)S(1)}, f32[2,136,1152]{2,1,0:T(8,128)}, u32[]{:S(2)}) copy-start(f32[2,136,1152]{2,1,0:T(8,128)} %get-tuple-element.703) | copy-start | bytes 3760132 | tf_op jit(solution)/shard_map/while
  48.2 1.9 copy-start.7
  48.3 2.2 %copy-start.1 = (f32[2,136,1152]{2,1,0:T(8,128)S(1)}, f32[2,136,1152]{2,1,0:T(8,128)}, u32[]{:S(2)}) copy-start(f32[2,136,1152]{2,1,0:T(8,128)} %get-tuple-element.702) | copy-start | bytes 3760132 | tf_op jit(solution)/shard_map/while
  48.3 2.5 %copy-start.3 = (f32[2,136,1152]{2,1,0:T(8,128)S(1)}, f32[2,136,1152]{2,1,0:T(8,128)}, u32[]{:S(2)}) copy-start(f32[2,136,1152]{2,1,0:T(8,128)} %get-tuple-element.703) | copy-start | bytes 3760132 | tf_op jit(solution)/shard_map/while
  61.9 1.9 copy-start.7
  62.0 2.2 %copy-start.1 = (f32[2,136,1152]{2,1,0:T(8,128)S(1)}, f32[2,136,1152]{2,1,0:T(8,128)}, u32[]{:S(2)}) copy-start(f32[2,136,1152]{2,1,0:T(8,128)} %get-tuple-element.702) | copy-start | bytes 3760132 | tf_op jit(solution)/shard_map/while
  62.0 2.5 %copy-start.3 = (f32[2,136,1152]{2,1,0:T(8,128)S(1)}, f32[2,136,1152]{2,1,0:T(8,128)}, u32[]{:S(2)}) copy-start(f32[2,136,1152]{2,1,0:T(8,128)} %get-tuple-element.703) | copy-start | bytes 3760132 | tf_op jit(solution)/shard_map/while
  75.8 2.2 %copy-start.1 = (f32[2,136,1152]{2,1,0:T(8,128)S(1)}, f32[2,136,1152]{2,1,0:T(8,128)}, u32[]{:S(2)}) copy-start(f32[2,136,1152]{2,1,0:T(8,128)} %get-tuple-element.702) | copy-start | bytes 3760132 | tf_op jit(solution)/shard_map/while
  75.8 2.5 %copy-start.3 = (f32[2,136,1152]{2,1,0:T(8,128)S(1)}, f32[2,136,1152]{2,1,0:T(8,128)}, u32[]{:S(2)}) copy-start(f32[2,136,1152]{2,1,0:T(8,128)} %get-tuple-element.703) | copy-start | bytes 3760132 | tf_op jit(solution)/shard_map/while
  89.5 2.2 %copy-start.1 = (f32[2,136,1152]{2,1,0:T(8,128)S(1)}, f32[2,136,1152]{2,1,0:T(8,128)}, u32[]{:S(2)}) copy-start(f32[2,136,1152]{2,1,0:T(8,128)} %get-tuple-element.702) | copy-start | bytes 3760132 | tf_op jit(solution)/shard_map/while
  89.5 2.5 %copy-start.3 = (f32[2,136,1152]{2,1,0:T(8,128)S(1)}, f32[2,136,1152]{2,1,0:T(8,128)}, u32[]{:S(2)}) copy-start(f32[2,136,1152]{2,1,0:T(8,128)} %get-tuple-element.703) | copy-start | bytes 3760132 | tf_op jit(solution)/shard_map/while
  103.2 2.2 %copy-start.1 = (f32[2,136,1152]{2,1,0:T(8,128)S(1)}, f32[2,136,1152]{2,1,0:T(8,128)}, u32[]{:S(2)}) copy-start(f32[2,136,1152]{2,1,0:T(8,128)} %get-tuple-element.702) | copy-start | bytes 3760132 | tf_op jit(solution)/shard_map/while
  103.2 2.5 %copy-start.3 = (f32[2,136,1152]{2,1,0:T(8,128)S(1)}, f32[2,136,1152]{2,1,0:T(8,128)}, u32[]{:S(2)}) copy-start(f32[2,136,1152]{2,1,0:T(8,128)} %get-tuple-element.703) | copy-start | bytes 3760132 | tf_op jit(solution)/shard_map/while
  116.8 1.9 copy-start.7
  116.9 2.2 %copy-start.1 = (f32[2,136,1152]{2,1,0:T(8,128)S(1)}, f32[2,136,1152]{2,1,0:T(8,128)}, u32[]{:S(2)}) copy-start(f32[2,136,1152]{2,1,0:T(8,128)} %get-tuple-element.702) | copy-start | bytes 3760132 | tf_op jit(solution)/shard_map/while
  117.0 2.5 %copy-start.3 = (f32[2,136,1152]{2,1,0:T(8,128)S(1)}, f32[2,136,1152]{2,1,0:T(8,128)}, u32[]{:S(2)}) copy-start(f32[2,136,1152]{2,1,0:T(8,128)} %get-tuple-element.703) | copy-start | bytes 3760132 | tf_op jit(solution)/shard_map/while
  130.7 2.2 %copy-start.1 = (f32[2,136,1152]{2,1,0:T(8,128)S(1)}, f32[2,136,1152]{2,1,0:T(8,128)}, u32[]{:S(2)}) copy-start(f32[2,136,1152]{2,1,0:T(8,128)} %get-tuple-element.702) | copy-start | bytes 3760132 | tf_op jit(solution)/shard_map/while
  130.7 2.5 %copy-start.3 = (f32[2,136,1152]{2,1,0:T(8,128)S(1)}, f32[2,136,1152]{2,1,0:T(8,128)}, u32[]{:S(2)}) copy-start(f32[2,136,1152]{2,1,0:T(8,128)} %get-tuple-element.703) | copy-start | bytes 3760132 | tf_op jit(solution)/shard_map/while
  144.4 2.2 %copy-start.1 = (f32[2,136,1152]{2,1,0:T(8,128)S(1)}, f32[2,136,1152]{2,1,0:T(8,128)}, u32[]{:S(2)}) copy-start(f32[2,136,1152]{2,1,0:T(8,128)} %get-tuple-element.702) | copy-start | bytes 3760132 | tf_op jit(solution)/shard_map/while
  144.4 2.5 %copy-start.3 = (f32[2,136,1152]{2,1,0:T(8,128)S(1)}, f32[2,136,1152]{2,1,0:T(8,128)}, u32[]{:S(2)}) copy-start(f32[2,136,1152]{2,1,0:T(8,128)} %get-tuple-element.703) | copy-start | bytes 3760132 | tf_op jit(solution)/shard_map/while
  158.7 8.8 %collective-permute-start.4 = (f32[9,16,512]{2,1,0:T(8,128)S(1)}, f32[9,16,512]{2,1,0:T(8,128)S(1)}, u32[]{:S(2)}, u32[]{:S(2)}) collective-permute-start(f32[9,16,512]{2,1,0:T(8,128)S(1)} %get-tuple-element.442), channel_id=1, source_target_pairs={{0,8},{8,16},{16,24},{24,0},{1,9},{9,17},{17,25},{25,1},{2,10},{10... | collective-permute-start | bytes 884744 | tf_op jit(solution)/shard_map/ppermute | solution.py:26
  160.0 25.5 %collective-permute-start.5 = (f32[9,16,512]{2,1,0:T(8,128)S(1)}, f32[9,16,512]{2,1,0:T(8,128)S(1)}, u32[]{:S(2)}, u32[]{:S(2)}) collective-permute-start(f32[9,16,512]{2,1,0:T(8,128)S(1)} %get-tuple-element.441), channel_id=1, source_target_pairs={{0,16},{8,24},{16,0},{24,8},{1,17},{9,25},{17,1},{25,9},{2,18},{10... | collective-permute-start | bytes 884744 | tf_op jit(solution)/shard_map/ppermute | solution.py:26
  161.0 26.5 %collective-permute-start.6 = (f32[9,16,512]{2,1,0:T(8,128)S(1)}, f32[9,16,512]{2,1,0:T(8,128)S(1)}, u32[]{:S(2)}, u32[]{:S(2)}) collective-permute-start(f32[9,16,512]{2,1,0:T(8,128)S(1)} %get-tuple-element.440), channel_id=1, source_target_pairs={{0,24},{8,0},{16,8},{24,16},{1,25},{9,1},{17,9},{25,17},{2,26},{10... | collective-permute-start | bytes 884744 | tf_op jit(solution)/shard_map/ppermute | solution.py:26
  (25 other events, 37.0 us)
